TPU v7x, 256 devices: a whole 4x4x8 slice. The times are simulated.
256 devices in a mesh: req: 32 (over y, z_hi, core), tp: 8 (over z_lo, x).
Axes of the slice: x: 4, y: 4, z: 8 (z_hi: 4, z_lo: 2; z = z_hi * 2 + z_lo), core: 2. Of those that a mesh axis runs over, the one named last changes fastest.
Arguments:
- tokens: bfloat16 [16384, 2048], P(('req', 'tp')), may hold values from -40 to 40, as said below
- attn_gain: float32 [2048], replicated, may hold values from 0.25 to 1.75
- w_query: bfloat16 [2048, 2048], P(None, 'tp'), may hold values from -0.125 to 0.125
- key_weight: bfloat16 [2048, 1024], P(None, 'tp'), may hold values from -0.125 to 0.125
- value_weight: bfloat16 [2048, 1024], P(None, 'tp'), may hold values from -0.125 to 0.125
- w_headgate: bfloat16 [2048, 16], P(None, 'tp'), may hold values from -0.125 to 0.125
- query_gain: float32 [128], replicated, may hold values from 1.3 to 2
- key_gain: float32 [128], replicated, may hold values from 1.3 to 2
- w_out: bfloat16 [2048, 2048], P('tp'), may hold values from -0.5 to 0.5
- mlp_gain: float32 [2048], replicated, may hold values from 0.25 to 1.75
- w_gate: bfloat16 [2048, 3072], P(None, 'tp'), may hold values from -0.125 to 0.125
- w_up: bfloat16 [2048, 3072], P(None, 'tp'), may hold values from -0.125 to 0.125
- w_down: bfloat16 [3072, 2048], P('tp'), may hold values from -0.109375 to 0.109375
- pooled_keys: bfloat16 [16384, 16, 8, 128], P(('req', 'tp')), may hold values from -150 to 150, as said below
- pooled_values: bfloat16 [16384, 16, 8, 128], P(('req', 'tp')), may hold values from -6 to 6
- sink_key_cache: bfloat16 [64, 4, 8, 128], P('req', None, 'tp'), may hold values from -12 to 12
- sink_value_cache: bfloat16 [64, 4, 8, 128], P('req', None, 'tp'), may hold values from -6 to 6
- cached_length: int32 [64], P('req'), may hold values from 0 to 32768, as said below
- valid_length: int32 [64], P('req'), may hold values from 1 to 256, as said below
- sink_position_count: int32 [64], P('req'), may hold values from 0 to 4, as said below
- window: int32 [64], P('req'), may hold values from 2048 to 4096, as said below
- page_slot: int32 [32, 512], P('req'), may hold values from 0 to 511, each once within a row
Outputs:
- out: float32 [16384, 2048], P(('req', 'tp'))
- app_keys: bfloat16 [16384, 8, 128], P('req', 'tp')
- app_values: bfloat16 [16384, 8, 128], P('req', 'tp')
Inputs may be any that keep to these rules, and one draw needn't show every extreme that they name: `tokens`: rows of the input; rows and features have unlike scales. `pooled_keys`: keys as the cache stores them. `cached_length`: short requests lie below 4096; some request has exactly 32768. `valid_length`: the rest of a span is padding; some request has exactly 256. `sink_position_count`: some request has exactly 4. `window`: some request has exactly 4096. `page_slot`: each row is a permutation.
All inputs are finite; a program needn't handle non-finite values.
Results may differ from a plain program's by a relative error of at most 0.02.
The roundings to bfloat16 on the way count: a program that leaves them out, or rounds other values in their place, can miss the bound.
Values may be sent and summed in bfloat16 or wider, within the bound.
A program may use at most 128 MiB of HBM per device.

v0:
```python
import math
import jax
import jax.numpy as jnp
from jax import lax
from jax.sharding import PartitionSpec as P

WINDOW_TOKENS = 4096
SPAN_TOKENS = 256
EPSILON = 1e-06
ROPE_BASE = 1000000.0
NEG_FILL = -1e30


def rms_rows(values, gain):
    mean_square = jnp.mean(values * values, axis=-1, keepdims=True)
    return values * lax.rsqrt(mean_square + EPSILON) * gain


def rotary(heads, positions):
    head_width = heads.shape[-1]
    half_width = head_width // 2
    freqs = ROPE_BASE ** (-2.0 * jnp.arange(half_width, dtype=jnp.float32) / head_width)
    angles = positions.astype(jnp.float32)[:, None] * freqs[None, :]
    cosine = jnp.cos(angles)[:, None, :]
    sine_part = jnp.sin(angles)[:, None, :]
    first_half = heads[..., :half_width]
    second_half = heads[..., half_width:]
    return jnp.concatenate(
        [
            first_half * cosine - second_half * sine_part,
            second_half * cosine + first_half * sine_part,
        ],
        axis=-1,
    )


def swiglu(normed_rows, w_gate, w_up):
    gate_part = jnp.dot(normed_rows, w_gate, preferred_element_type=jnp.float32)
    up_part = jnp.dot(normed_rows, w_up, preferred_element_type=jnp.float32)
    return (jax.nn.silu(gate_part) * up_part).astype(jnp.bfloat16)


def masked_max(scores, allowed):
    return jnp.max(jnp.where(allowed, scores, NEG_FILL), axis=-1)


def near_masks(cached, valid, sinks_used, reach, span_len, window_len, sink_len):
    offsets = jnp.arange(span_len, dtype=jnp.int32)
    sink_slots = jnp.arange(sink_len, dtype=jnp.int32)
    sink_ok = (sink_slots[None, :] < sinks_used[:, None]) & (
        sink_slots[None, :] < (cached - window_len)[:, None]
    )
    span_ok = (
        (offsets[None, None, :] < valid[:, None, None])
        & (offsets[None, None, :] <= offsets[None, :, None])
        & (
            (cached[:, None, None] + offsets[None, None, :] < sinks_used[:, None, None])
            | (offsets[None, :, None] - offsets[None, None, :] <= reach[:, None, None])
        )
    )
    return (sink_ok[:, None, None, None, :], span_ok[:, :, None, None, :])


def near_scores(query_vectors, sink_key_rows, fresh_keys, score_scale):
    sink_scores = (
        jnp.einsum(
            "rckgd,rskd->rckgs", query_vectors, sink_key_rows, preferred_element_type=jnp.float32
        )
        * score_scale
    )
    span_scores = (
        jnp.einsum(
            "rckgd,rtkd->rckgt", query_vectors, fresh_keys, preferred_element_type=jnp.float32
        )
        * score_scale
    )
    return (sink_scores, span_scores)


def attend_whole(
    query_vectors,
    sink_key_rows,
    sink_value_rows,
    window_key_rows,
    window_value_rows,
    fresh_keys,
    fresh_values,
    cached,
    valid,
    sinks_used,
    reach,
    score_scale,
):
    span_len = query_vectors.shape[1]
    window_len = window_key_rows.shape[1]
    sink_ok, span_ok = near_masks(
        cached, valid, sinks_used, reach, span_len, window_len, sink_key_rows.shape[1]
    )
    offsets = jnp.arange(span_len, dtype=jnp.int32)
    window_slots = jnp.arange(window_len, dtype=jnp.int32)
    key_positions = cached[:, None] - window_len + window_slots[None, :]
    window_ok = (key_positions[:, None, :] >= 0) & (
        (key_positions[:, None, :] < sinks_used[:, None, None])
        | (
            (window_len - window_slots)[None, None, :] + offsets[None, :, None]
            <= reach[:, None, None]
        )
    )
    window_ok = window_ok[:, :, None, None, :]
    sink_scores, span_scores = near_scores(query_vectors, sink_key_rows, fresh_keys, score_scale)
    window_scores = (
        jnp.einsum(
            "rckgd,rwkd->rckgw", query_vectors, window_key_rows, preferred_element_type=jnp.float32
        )
        * score_scale
    )
    highest = jnp.maximum(
        jnp.maximum(masked_max(sink_scores, sink_ok), masked_max(window_scores, window_ok)),
        masked_max(span_scores, span_ok),
    )[..., None]
    sink_weights = jnp.where(sink_ok, jnp.exp(sink_scores - highest), 0.0)
    window_weights = jnp.where(window_ok, jnp.exp(window_scores - highest), 0.0)
    span_weights = jnp.where(span_ok, jnp.exp(span_scores - highest), 0.0)
    total = (
        jnp.sum(sink_weights, axis=-1)
        + jnp.sum(window_weights, axis=-1)
        + jnp.sum(span_weights, axis=-1)
    )
    summed = jnp.einsum(
        "rckgs,rskd->rckgd",
        sink_weights.astype(jnp.bfloat16),
        sink_value_rows,
        preferred_element_type=jnp.float32,
    )
    summed = summed + jnp.einsum(
        "rckgw,rwkd->rckgd",
        window_weights.astype(jnp.bfloat16),
        window_value_rows,
        preferred_element_type=jnp.float32,
    )
    summed = summed + jnp.einsum(
        "rckgt,rtkd->rckgd",
        span_weights.astype(jnp.bfloat16),
        fresh_values,
        preferred_element_type=jnp.float32,
    )
    return summed / total[..., None]


def body(
    tokens,
    attn_gain,
    w_query,
    key_weight,
    value_weight,
    w_headgate,
    query_gain,
    key_gain,
    w_out,
    mlp_gain,
    w_gate,
    w_up,
    w_down,
    pooled_keys,
    pooled_values,
    sink_key_cache,
    sink_value_cache,
    cached_length,
    valid_length,
    sink_position_count,
    window,
    page_slot,
):
    head_dim = query_gain.shape[0]
    heads_dev = w_query.shape[1] // head_dim
    kv_dev = key_weight.shape[1] // head_dim
    group_size = heads_dev // kv_dev
    requests_dev = cached_length.shape[0]
    window_len = WINDOW_TOKENS
    span_len = SPAN_TOKENS
    rows_own = tokens.shape[0]
    score_scale = 1.0 / math.sqrt(head_dim)
    tp_index = lax.axis_index("tp")
    all_rows = lax.all_gather(tokens, "tp", axis=0, tiled=True)
    residual = all_rows.astype(jnp.float32)
    normalized_input = rms_rows(residual, attn_gain).astype(jnp.bfloat16)
    rows_total = normalized_input.shape[0]
    offsets = jnp.arange(span_len, dtype=jnp.int32)
    positions = (cached_length[:, None] + offsets[None, :]).reshape(rows_total)
    query_vectors = jnp.dot(normalized_input, w_query, preferred_element_type=jnp.float32).reshape(
        rows_total, heads_dev, head_dim
    )
    query_vectors = rotary(rms_rows(query_vectors, query_gain), positions).astype(jnp.bfloat16)
    fresh_keys = jnp.dot(normalized_input, key_weight, preferred_element_type=jnp.float32).reshape(
        rows_total, kv_dev, head_dim
    )
    fresh_keys = rotary(rms_rows(fresh_keys, key_gain), positions).astype(jnp.bfloat16)
    fresh_values = (
        jnp.dot(normalized_input, value_weight, preferred_element_type=jnp.float32)
        .astype(jnp.bfloat16)
        .reshape(rows_total, kv_dev, head_dim)
    )
    headgate = jax.nn.sigmoid(
        jnp.dot(normalized_input, w_headgate, preferred_element_type=jnp.float32)
    )
    present = (offsets[None, :] < valid_length[:, None]).reshape(rows_total)[:, None, None]
    app_keys = jnp.where(present, fresh_keys, jnp.zeros_like(fresh_keys))
    app_values = jnp.where(present, fresh_values, jnp.zeros_like(fresh_values))
    query_blocks = query_vectors.reshape(requests_dev, span_len, kv_dev, group_size, head_dim)
    key_blocks = fresh_keys.reshape(requests_dev, span_len, kv_dev, head_dim)
    value_blocks = fresh_values.reshape(requests_dev, span_len, kv_dev, head_dim)
    arrived_keys, arrived_values = (
        lax.all_to_all(pooled_keys, "tp", split_axis=2, concat_axis=0, tiled=True),
        lax.all_to_all(pooled_values, "tp", split_axis=2, concat_axis=0, tiled=True),
    )
    window_key_rows = jnp.take(arrived_keys, page_slot[0], axis=0).reshape(
        requests_dev, window_len, kv_dev, head_dim
    )
    window_value_rows = jnp.take(arrived_values, page_slot[0], axis=0).reshape(
        requests_dev, window_len, kv_dev, head_dim
    )
    mixture = attend_whole(
        query_blocks,
        sink_key_cache,
        sink_value_cache,
        window_key_rows,
        window_value_rows,
        key_blocks,
        value_blocks,
        cached_length,
        valid_length,
        sink_position_count,
        window,
        score_scale,
    )
    mixture = mixture.reshape(rows_total, heads_dev, head_dim)
    heads_out = (
        (mixture * headgate[..., None])
        .astype(jnp.bfloat16)
        .reshape(rows_total, heads_dev * head_dim)
    )
    attn = lax.psum(
        jnp.dot(heads_out, w_out, preferred_element_type=jnp.float32).astype(jnp.bfloat16), "tp"
    ).astype(jnp.float32)
    middle = residual + attn
    hidden = swiglu(rms_rows(middle, mlp_gain).astype(jnp.bfloat16), w_gate, w_up)
    branch = lax.psum(
        jnp.dot(hidden, w_down, preferred_element_type=jnp.float32).astype(jnp.bfloat16), "tp"
    ).astype(jnp.float32)
    row_start = tp_index * rows_own
    output = lax.dynamic_slice_in_dim(middle, row_start, rows_own, 0) + lax.dynamic_slice_in_dim(
        branch, row_start, rows_own, 0
    )
    return (output, app_keys, app_values)


def solution(mesh):
    in_specs = (
        P(("req", "tp"), None),
        P(),
        P(None, "tp"),
        P(None, "tp"),
        P(None, "tp"),
        P(None, "tp"),
        P(),
        P(),
        P("tp", None),
        P(),
        P(None, "tp"),
        P(None, "tp"),
        P("tp", None),
        P(("req", "tp"), None, None, None),
        P(("req", "tp"), None, None, None),
        P("req", None, "tp", None),
        P("req", None, "tp", None),
        P("req"),
        P("req"),
        P("req"),
        P("req"),
        P("req", None),
    )
    out_specs = (P(("req", "tp"), None), P("req", "tp", None), P("req", "tp", None))
    return jax.shard_map(body, mesh=mesh, in_specs=in_specs, out_specs=out_specs, check_vma=False)
```

profile of v0, /device:TPU:8, one launch (start us, length us, event | category | flops | bytes accessed | tf_op | source)
XLA Modules:
  0.0 337.1 jit_solution(11308946592861896893)
XLA Ops:
  7.9 3.2 copy.39
  11.1 5.8 %all-to-all-start.1 = ((bf16[64,16,8,128]{3,1,0,2:T(8,128)(2,1)}), bf16[64,16,8,128]{3,1,0,2:T(8,128)(2,1)}, u32[]{:S(2)}, u32[]{:S(2)}) async-start(bf16[64,16,8,128]{3,1,0,2:T(8,128)(2,1)} %copy.39), calls=%async_computation.1 | async-start | bytes 4194304 | tf_op jit(solution)/shard_map/all_to_all | solution.py:214
  17.2 3.2 copy.36
  22.0 4.6 %or_and_fusion = pred[2,256,4096]{1,2,0:T(8,128)(4,1)} fusion(s32[256,4096]{0,1:T(8,128)S(1)} %iota_add_fusion, s32[2]{0:T(128)S(1)} %copy-done.16, pred[2,4096]{1,0:T(4,128)(4,1)S(1)} %get-tuple-element.21, pred[2,4096]{1,0:T(4,128)(4,1)S(1)} %get-tuple-element.20), kind=kLoop, calls=%fused_computation.12 | loop fusion | flops 6291456 | bytes 6307848 | tf_op jit(solution)/shard_map/and | solution.py:102
  26.5 22.6 %all-to-all-done.1 = bf16[64,16,8,128]{3,1,0,2:T(8,128)(2,1)} async-done(((bf16[64,16,8,128]{3,1,0,2:T(8,128)(2,1)}), bf16[64,16,8,128]{3,1,0,2:T(8,128)(2,1)}, u32[]{:S(2)}, u32[]{:S(2)}) %all-to-all-start.1) | async-done | bytes 2097184 | tf_op jit(solution)/shard_map/all_to_all | solution.py:214
  49.1 5.7 %all-to-all-start = ((bf16[64,16,8,128]{3,1,0,2:T(8,128)(2,1)}), bf16[64,16,8,128]{3,1,0,2:T(8,128)(2,1)}, u32[]{:S(2)}, u32[]{:S(2)}) async-start(bf16[64,16,8,128]{3,1,0,2:T(8,128)(2,1)} %copy.36), calls=%async_computation | async-start | bytes 4194304 | tf_op jit(solution)/shard_map/all_to_all | solution.py:213
  54.9 30.4 %all-gather.2.cloned.1.call-done = bf16[512,2048]{1,0:T(8,128)(2,1)} async-done(((bf16[64,2048]{1,0:T(8,128)(2,1)}), bf16[512,2048]{1,0:T(8,128)(2,1)}) %all-gather.2.cloned.1.call-update) | async-done | bytes 2097168 | tf_op jit(solution)/shard_map/all_gather | solution.py:184
  85.4 2.2 fusion.9
  90.4 2.6 multiply_reduce_fusion.1
  94.1 2.4 multiply_reduce_fusion.2
  97.4 4.0 %gather_fusion.1 = bf16[512,16,128]{2,1,0:T(8,128)(2,1)} fusion(bf16[512,16,128]{2,1,0:T(8,128)(2,1)} %bitcast.34, s32[1024]{0:T(1024)S(1)} %pad_clamp_fusion), kind=kCustom, calls=%fused_computation.1.clone | custom fusion | bytes 4196352 | tf_op jit(solution)/shard_map/jit(_take)/gather | solution.py:219
  101.5 2.3 convolution_convert_fusion.2
  103.8 4.0 %gather_fusion = bf16[512,16,128]{2,1,0:T(8,128)(2,1)} fusion(bf16[512,16,128]{2,1,0:T(8,128)(2,1)} %bitcast.11, s32[1024]{0:T(1024)S(1)} %pad_clamp_fusion), kind=kCustom, calls=%fused_computation.clone | custom fusion | bytes 4196352 | tf_op jit(solution)/shard_map/jit(_take)/gather | solution.py:216
  107.8 4.9 %bitcast_select_fusion.1 = (bf16[512,16,1,128]{3,1,0,2:T(8,128)(2,1)}, bf16[512,16,1,128]{3,1,0,2:T(8,128)(2,1)}) fusion(bf16[512,16,128]{2,1,0:T(8,128)(2,1)} %gather_fusion.1, pred[512]{0:T(512)(128)(4,1)S(1)} %compare_and_fusion, bf16[512,16,128]{2,1,0:T(8,128)(2,1)} %gather_fusion), kind=kLoop, calls=%fused_computation.24 | loop fusion | flops 2097152 | bytes 8389120 | tf_op jit(solution)/shard_map/jit(_take)/select_n | solution.py:219
  112.9 4.1 %fusion = (f32[2,256,2]{1,2,0:T(2,128)S(1)}, f32[2,4096,256,2]{2,1,3,0:T(8,128)S(1)}) fusion(pred[2,256,4096]{1,2,0:T(8,128)(4,1)S(1)} %copy-done.5, bf16[2,4096,128,1]{2,1,3,0:T(8,128)(2,1)} %bitcast.160, bf16[2,256,2,64]{3,1,2,0:T(8,128)(2,1)S(1)} %copy.35, bf16[2,256,2,64]{3,1,2,0:T(8,128)(2,1)S(1)} %copy.34), kind=kOutput, calls=%fused_computation.4 | convolution fusion | flops 1086848000 | bytes 21237760 | tf_op jit(solution)/shard_map/rckgd,rwkd->rckgw/dot_general | solution.py:112
  118.1 3.9 %fusion.3 = f32[2,256,2]{1,2,0:T(2,128)S(1)} fusion(f32[2,4096,256,2]{2,1,3,0:T(8,128)S(1)} %get-tuple-element.31, f32[2,256,2]{1,2,0:T(2,128)S(1)} %maximum_maximum_fusion, pred[2,256,4096]{1,2,0:T(8,128)(4,1)S(1)} %copy-done.5), kind=kLoop, calls=%fused_computation.7 | loop fusion | flops 16776192 | bytes 18882560 | tf_op jit(solution)/shard_map/reduce_sum | solution.py:126
  122.8 9.7 %fusion.6 = f32[2,128,256,2]{1,2,3,0:T(8,128)S(1)} fusion(bf16[2,4096,128,1]{2,1,3,0:T(8,128)(2,1)} %bitcast.159, f32[2,4096,256,2]{2,1,3,0:T(8,128)} %copy-done.4, f32[2,256,2]{1,2,0:T(2,128)S(1)} %maximum_maximum_fusion, pred[2,256,4096]{1,2,0:T(8,128)(4,1)} %or_and_fusion), kind=kOutput, calls=%fused_computation.10 | convolution fusion | flops 1090519040 | bytes 21499904 | tf_op jit(solution)/shard_map/rckgw,rwkd->rckgd/dot_general | solution.py:135
  134.0 2.0 convolution_convert_fusion
  136.4 90.3 %all-reduce.3.cloned.1.call-done = bf16[512,2048]{1,0:T(8,128)(2,1)} async-done(((bf16[512,2048]{1,0:T(8,128)(2,1)}), bf16[512,2048]{1,0:T(8,128)(2,1)}) %all-reduce.3.cloned.1.call-update) | async-done | bytes 2097168 | tf_op jit(solution)/shard_map/psum | solution.py:242
  226.6 5.0 %multiply_reduce_fusion = (f32[512]{0:T(512)S(1)}, f32[512,2048]{1,0:T(8,128)}) fusion(bf16[512,2048]{1,0:T(8,128)(2,1)} %all-reduce.3.cloned.1.call-done, bf16[512,2048]{1,0:T(8,128)(2,1)} %all-gather.2.cloned.1.call-done), kind=kLoop, calls=%fused_computation.20 | loop fusion | flops 5242368 | bytes 8390656 | tf_op jit(solution)/shard_map/reduce_sum | solution.py:15
  231.7 2.7 fusion.66
  234.4 6.4 %convolution_convert_fusion.1 = bf16[512,2048]{1,0:T(8,128)(2,1)} fusion(bf16[384,2048]{1,0:T(8,128)(2,1)S(1)} %copy-done, bf16[2048,384]{1,0:T(8,128)(2,1)} %param.35, f32[512,384]{1,0:T(8,128)S(1)} %fusion.66, f32[2048]{0:T(1024)S(1)} %copy-done.20, f32[512]{0:T(512)S(1)} %add_rsqrt_fusion.1, bf16[512,2048]{1,0:T(8,128)(2,1)} %all-gather.2.cloned.1.call-done, ...), kind=kOutput, calls=%fused_computation.23 | convolution fusion | flops 1619132416 | bytes 10233856 | tf_op jit(solution)/shard_map/dot_general | solution.py:248
  242.4 86.2 %all-reduce.5.cloned.1.call-done = bf16[512,2048]{1,0:T(8,128)(2,1)} async-done(((bf16[512,2048]{1,0:T(8,128)(2,1)}), bf16[512,2048]{1,0:T(8,128)(2,1)}) %all-reduce.5.cloned.1.call-update) | async-done | bytes 2097168 | tf_op jit(solution)/shard_map/psum | solution.py:247
  328.6 1.9 convert_add_fusion.1
  (98 shorter events, 12.7 us)
Async XLA Ops:
  7.2 227.2 %copy-start = (bf16[384,2048]{1,0:T(8,128)(2,1)S(1)}, bf16[384,2048]{1,0:T(8,128)(2,1)}, u32[]{:S(2)}) copy-start(bf16[384,2048]{1,0:T(8,128)(2,1)} %param.36) | copy-start | bytes 4718596
  7.2 78.2 %all-gather.2.cloned.1.call-start = ((), (), s32[]{:S(2)}) async-start(), calls=%async_computation.2 | async-start | bytes 2359296 | tf_op jit(solution)/shard_map/all_gather | solution.py:184
  11.1 5.8 %copy-start.15 = (s32[2]{0:T(128)S(1)}, s32[2]{0:T(128)}, u32[]{:S(2)}) copy-start(s32[2]{0:T(128)} %param.41) | copy-start | bytes 28
  11.1 5.9 %copy-start.12 = (s32[1,512]{1,0:T(1,128)S(1)}, s32[1,512]{1,0:T(1,128)}, u32[]{:S(2)}) copy-start(s32[1,512]{1,0:T(1,128)} %param.45) | copy-start | bytes 6148
  11.1 5.9 %copy-start.14 = (s32[2]{0:T(128)S(1)}, s32[2]{0:T(128)}, u32[]{:S(2)}) copy-start(s32[2]{0:T(128)} %param.43) | copy-start | bytes 28
  11.1 6.0 %copy-start.19 = (s32[2]{0:T(128)S(1)}, s32[2]{0:T(128)}, u32[]{:S(2)}) copy-start(s32[2]{0:T(128)} %param.42) | copy-start | bytes 28
  11.1 38.0 %all-to-all-start.1 = ((bf16[64,16,8,128]{3,1,0,2:T(8,128)(2,1)}), bf16[64,16,8,128]{3,1,0,2:T(8,128)(2,1)}, u32[]{:S(2)}, u32[]{:S(2)}) async-start(bf16[64,16,8,128]{3,1,0,2:T(8,128)(2,1)} %copy.39), calls=%async_computation.1 | async-start | bytes 4194304 | tf_op jit(solution)/shard_map/all_to_all | solution.py:214
  17.2 3.8 %copy-start.16 = (s32[2]{0:T(128)S(1)}, s32[2]{0:T(128)}, u32[]{:S(2)}) copy-start(s32[2]{0:T(128)} %param.44) | copy-start | bytes 28
  49.1 54.6 %all-to-all-start = ((bf16[64,16,8,128]{3,1,0,2:T(8,128)(2,1)}), bf16[64,16,8,128]{3,1,0,2:T(8,128)(2,1)}, u32[]{:S(2)}, u32[]{:S(2)}) async-start(bf16[64,16,8,128]{3,1,0,2:T(8,128)(2,1)} %copy.36), calls=%async_computation | async-start | bytes 4194304 | tf_op jit(solution)/shard_map/all_to_all | solution.py:213
  54.9 32.7 %copy-start.10 = (f32[2048]{0:T(1024)S(1)}, f32[2048]{0:T(1024)}, u32[]{:S(2)}) copy-start(f32[2048]{0:T(1024)} %param.25) | copy-start | bytes 24580
  54.9 171.7 %all-reduce.3.cloned.1.call-start = ((), (), s32[]{:S(2)}) async-start(), calls=%async_computation.3 | async-start | bytes 4194304 | tf_op jit(solution)/shard_map/psum | solution.py:242
  85.3 2.2 copy-start.2
  87.6 1.9 copy-start.11
  90.2 2.8 copy-start.17
  93.3 3.2 copy-start.18
  97.4 4.1 %copy-start.9 = (bf16[2048,128]{1,0:T(8,128)(2,1)S(1)}, bf16[2048,128]{1,0:T(8,128)(2,1)}, u32[]{:S(2)}) copy-start(bf16[2048,128]{1,0:T(8,128)(2,1)} %param.28) | copy-start | bytes 1572868
  107.8 4.9 %copy-start.13 = (bf16[2,4,1,128]{3,1,2,0:T(4,128)(2,1)S(1)}, bf16[2,4,1,128]{3,1,2,0:T(4,128)(2,1)}, u32[]{:S(2)}) copy-start(bf16[2,4,1,128]{3,1,2,0:T(4,128)(2,1)} %param.39) | copy-start | bytes 6148
  107.8 5.2 %copy-start.5 = (pred[2,256,4096]{1,2,0:T(8,128)(4,1)S(1)}, pred[2,256,4096]{1,2,0:T(8,128)(4,1)}, u32[]{:S(2)}) copy-start(pred[2,256,4096]{1,2,0:T(8,128)(4,1)} %or_and_fusion) | copy-start | bytes 6291460
  117.0 5.7 %copy-start.4 = (f32[2,4096,256,2]{2,1,3,0:T(8,128)}, f32[2,4096,256,2]{2,1,3,0:T(8,128)S(1)}, u32[]{:S(2)}) copy-start(f32[2,4096,256,2]{2,1,3,0:T(8,128)S(1)} %get-tuple-element.31) | copy-start | bytes 50331652
  122.8 9.8 %copy-start.21 = (bf16[2,4,1,128]{3,1,2,0:T(4,128)(2,1)S(1)}, bf16[2,4,1,128]{3,1,2,0:T(4,128)(2,1)}, u32[]{:S(2)}) copy-start(bf16[2,4,1,128]{3,1,2,0:T(4,128)(2,1)} %param.40) | copy-start | bytes 6148
  136.1 95.6 %copy-start.20 = (f32[2048]{0:T(1024)S(1)}, f32[2048]{0:T(1024)}, u32[]{:S(2)}) copy-start(f32[2048]{0:T(1024)} %param.33) | copy-start | bytes 24580
  136.1 192.5 %all-reduce.5.cloned.1.call-start = ((), (), s32[]{:S(2)}) async-start(), calls=%async_computation.4 | async-start | bytes 4194304 | tf_op jit(solution)/shard_map/psum | solution.py:247
  226.6 5.0 %copy-start.3 = (bf16[512,2048]{1,0:T(8,128)(2,1)S(1)}, bf16[512,2048]{1,0:T(8,128)(2,1)}, u32[]{:S(2)}) copy-start(bf16[512,2048]{1,0:T(8,128)(2,1)} %all-gather.2.cloned.1.call-done) | copy-start | bytes 6291460
  226.6 5.0 %copy-start.6 = (bf16[512,2048]{1,0:T(8,128)(2,1)S(1)}, bf16[512,2048]{1,0:T(8,128)(2,1)}, u32[]{:S(2)}) copy-start(bf16[512,2048]{1,0:T(8,128)(2,1)} %all-reduce.3.cloned.1.call-done) | copy-start | bytes 6291460
  (3 other events, 4.0 us)
Sparse Core Ops, SparseCore 0:
  9.8 75.5 all-gather.1
  136.2 90.3 all-reduce.2
  241.0 87.5 all-reduce.4
where the time goes:
time: 338 us; the launch traced here: 337 us
  waiting for transfers between devices  230 us (68%)
  matrix products  34.5 us (10%)
  other arithmetic  26.8 us (8%)
  local copies, waits for them, and re-layouts  19.5 us (6%)
  between operations  14.2 us (4%)
  starting transfers between devices  11.9 us (4%)
    psum x1, waiting for transfers between devices, body(): lax.psum(jnp.dot(heads_out, w_out, preferred_element_type=jnp.float32).as...  90.3 us
    psum x1, waiting for transfers between devices, body(): lax.psum(jnp.dot(hidden, w_down, preferred_element_type=jnp.float32).asty...  86.2 us
    all_gather x1, waiting for transfers between devices, body(): all_rows = lax.all_gather(tokens, 'tp', axis=0, tiled=True)  30.4 us
    all_to_all x1, waiting for transfers between devices, body(): lax.all_to_all(pooled_values, 'tp', split_axis=2, concat_axis=0, tiled=True)  22.6 us
    dot_general x1, matrix products, attend_whole(): jnp.einsum('rckgw,rwkd->rckgd', window_weights.astype(jnp.bfloat16), wind...  9.68 us
    unnamed x48, local copies, waits for them, and re-layouts  9.65 us
    reduce_sum x2, other arithmetic, rms_rows(): mean_square = jnp.mean(values * values, axis=-1, keepdims=True)  7.22 us
  transfers between devices with their start and end apart: 5, of which 4 were waited for; matrix products, arithmetic and copies ran while one was open for 9% of the time, Pallas kernels for 0%

commit v1 on v0

--- a/solution.py
+++ b/solution.py
@@ -239,8 +239,11 @@
         .astype(jnp.bfloat16)
         .reshape(rows_total, heads_dev * head_dim)
     )
-    attn = lax.psum(
-        jnp.dot(heads_out, w_out, preferred_element_type=jnp.float32).astype(jnp.bfloat16), "tp"
+    attn = jnp.sum(
+        lax.all_gather(
+            jnp.dot(heads_out, w_out, preferred_element_type=jnp.float32).astype(jnp.bfloat16), "tp"
+        ),
+        axis=0,
     ).astype(jnp.float32)
     middle = residual + attn
     hidden = swiglu(rms_rows(middle, mlp_gain).astype(jnp.bfloat16), w_gate, w_up)

time: 338 us -> 431 us (1.28)
  waiting for transfers between devices: 230 us -> 315 us
  other arithmetic: 26.8 us -> 37.9 us
    all_gather x0 -> x1, waiting for transfers between devices: none -> 176 us  [body(): lax.all_gather(jnp.dot(heads_out, w_out, preferred_element_type=jnp.float...]
    psum x1 -> x0, waiting for transfers between devices: 90.3 us -> none  [body(): lax.psum(jnp.dot(heads_out, w_out, preferred_element_type=jnp.float32).as...]
    reduce_sum x0 -> x1, other arithmetic: none -> 11 us  [body(): jnp.sum(lax.all_gather(jnp.dot(heads_out, w_out, preferred_element_type=j...]
    unnamed x48 -> x50, local copies, waits for them, and re-layouts: 9.65 us -> 9.64 us
  transfers between devices with their start and end apart: 5 -> 5, of which waited for: 4 -> 4; matrix products, arithmetic and copies ran while one was open for 9% -> 7% of each run, Pallas kernels for 0% -> 0%
where the time goes in v1:
time: 431 us
  waiting for transfers between devices  315 us (73%)
  other arithmetic  37.9 us (9%)
  matrix products  33 us (8%)
  local copies, waits for them, and re-layouts  19.5 us (5%)
  between operations  14.2 us (3%)
  starting transfers between devices  11.6 us (3%)
    all_gather x1, waiting for transfers between devices, body(): lax.all_gather(jnp.dot(heads_out, w_out, preferred_element_type=jnp.float...  176 us
    psum x1, waiting for transfers between devices, body(): lax.psum(jnp.dot(hidden, w_down, preferred_element_type=jnp.float32).asty...  84.6 us
    all_gather x1, waiting for transfers between devices, body(): all_rows = lax.all_gather(tokens, 'tp', axis=0, tiled=True)  30.4 us
    all_to_all x1, waiting for transfers between devices, body(): lax.all_to_all(pooled_values, 'tp', split_axis=2, concat_axis=0, tiled=True)  22.6 us
    reduce_sum x1, other arithmetic, body(): jnp.sum(lax.all_gather(jnp.dot(heads_out, w_out, preferred_element_type=j...  11 us
    dot_general x1, matrix products, attend_whole(): jnp.einsum('rckgw,rwkd->rckgd', window_weights.astype(jnp.bfloat16), wind...  9.67 us
    unnamed x50, local copies, waits for them, and re-layouts  9.64 us
  transfers between devices with their start and end apart: 5, of which 4 were waited for; matrix products, arithmetic and copies ran while one was open for 7% of the time, Pallas kernels for 0%

profile of v1, /device:TPU:8, one launch (start us, length us, event | category | flops | bytes accessed | tf_op | source)
XLA Modules:
  0.0 430.8 jit_solution(2428506700778408653)
XLA Ops:
  7.9 3.2 copy.39
  11.1 5.8 %all-to-all-start.1 = ((bf16[64,16,8,128]{3,1,0,2:T(8,128)(2,1)}), bf16[64,16,8,128]{3,1,0,2:T(8,128)(2,1)}, u32[]{:S(2)}, u32[]{:S(2)}) async-start(bf16[64,16,8,128]{3,1,0,2:T(8,128)(2,1)} %copy.39), calls=%async_computation.1 | async-start | bytes 4194304 | tf_op jit(solution)/shard_map/all_to_all | solution.py:214
  17.2 3.2 copy.36
  22.0 4.6 %or_and_fusion = pred[2,256,4096]{1,2,0:T(8,128)(4,1)} fusion(s32[256,4096]{0,1:T(8,128)S(1)} %iota_add_fusion, s32[2]{0:T(128)S(1)} %copy-done.16, pred[2,4096]{1,0:T(4,128)(4,1)S(1)} %get-tuple-element.21, pred[2,4096]{1,0:T(4,128)(4,1)S(1)} %get-tuple-element.20), kind=kLoop, calls=%fused_computation.12 | loop fusion | flops 6291456 | bytes 6307848 | tf_op jit(solution)/shard_map/and | solution.py:102
  26.6 22.6 %all-to-all-done.1 = bf16[64,16,8,128]{3,1,0,2:T(8,128)(2,1)} async-done(((bf16[64,16,8,128]{3,1,0,2:T(8,128)(2,1)}), bf16[64,16,8,128]{3,1,0,2:T(8,128)(2,1)}, u32[]{:S(2)}, u32[]{:S(2)}) %all-to-all-start.1) | async-done | bytes 2097184 | tf_op jit(solution)/shard_map/all_to_all | solution.py:214
  49.1 5.7 %all-to-all-start = ((bf16[64,16,8,128]{3,1,0,2:T(8,128)(2,1)}), bf16[64,16,8,128]{3,1,0,2:T(8,128)(2,1)}, u32[]{:S(2)}, u32[]{:S(2)}) async-start(bf16[64,16,8,128]{3,1,0,2:T(8,128)(2,1)} %copy.36), calls=%async_computation | async-start | bytes 4194304 | tf_op jit(solution)/shard_map/all_to_all | solution.py:213
  54.9 30.4 %all-gather.4.cloned.1.call-done = bf16[512,2048]{1,0:T(8,128)(2,1)} async-done(((bf16[64,2048]{1,0:T(8,128)(2,1)}), bf16[512,2048]{1,0:T(8,128)(2,1)}) %all-gather.4.cloned.1.call-update) | async-done | bytes 2097168 | tf_op jit(solution)/shard_map/all_gather | solution.py:184
  85.3 2.2 fusion.9
  90.4 2.6 multiply_reduce_fusion.1
  94.0 2.4 multiply_reduce_fusion.2
  97.4 4.0 gather_fusion.1
  101.5 2.3 convolution_convert_fusion.2
  103.8 4.0 gather_fusion
  107.7 4.9 %bitcast_select_fusion.1 = (bf16[512,16,1,128]{3,1,0,2:T(8,128)(2,1)}, bf16[512,16,1,128]{3,1,0,2:T(8,128)(2,1)}) fusion(bf16[512,16,128]{2,1,0:T(8,128)(2,1)} %gather_fusion.1, pred[512]{0:T(512)(128)(4,1)S(1)} %compare_and_fusion, bf16[512,16,128]{2,1,0:T(8,128)(2,1)} %gather_fusion), kind=kLoop, calls=%fused_computation.24 | loop fusion | flops 2097152 | bytes 8389120 | tf_op jit(solution)/shard_map/jit(_take)/select_n | solution.py:219
  112.9 4.1 fusion
  118.1 3.9 fusion.3
  122.7 9.7 %fusion.6 = f32[2,128,256,2]{1,2,3,0:T(8,128)S(1)} fusion(bf16[2,4096,128,1]{2,1,3,0:T(8,128)(2,1)} %bitcast.161, f32[2,4096,256,2]{2,1,3,0:T(8,128)} %copy-done.4, f32[2,256,2]{1,2,0:T(2,128)S(1)} %maximum_maximum_fusion, pred[2,256,4096]{1,2,0:T(8,128)(4,1)} %or_and_fusion), kind=kOutput, calls=%fused_computation.10 | convolution fusion | flops 1090519040 | bytes 21499904 | tf_op jit(solution)/shard_map/rckgw,rwkd->rckgd/dot_general | solution.py:135
  134.0 2.0 convolution_convert_fusion
  136.1 176.2 %all-gather.6.cloned.1.call-done = bf16[4096,2048]{1,0:T(8,128)(2,1)} async-done(((bf16[512,2048]{1,0:T(8,128)(2,1)}), bf16[4096,2048]{1,0:T(8,128)(2,1)}) %all-gather.6.cloned.1.call-update) | async-done | bytes 16777232 | tf_op jit(solution)/shard_map/all_gather | solution.py:243
  312.3 11.0 %reduce_sum.81 = bf16[512,2048]{1,0:T(8,128)(2,1)} reduce(bf16[8,512,2048]{2,1,0:T(8,128)(2,1)} %bitcast.160, bf16[]{:T(256)} %constant.38.clone.1), dimensions={0}, to_apply=%region_9.11 | reduce | flops 7340032 | bytes 18874370 | tf_op jit(solution)/shard_map/reduce_sum | solution.py:242
  323.3 5.0 %multiply_reduce_fusion = (f32[512]{0:T(512)S(1)}, f32[512,2048]{1,0:T(8,128)}) fusion(bf16[512,2048]{1,0:T(8,128)(2,1)} %reduce_sum.81, bf16[512,2048]{1,0:T(8,128)(2,1)} %all-gather.4.cloned.1.call-done), kind=kLoop, calls=%fused_computation.20 | loop fusion | flops 5242368 | bytes 8390656 | tf_op jit(solution)/shard_map/reduce_sum | solution.py:15
  329.6 6.4 %convolution_convert_fusion.1 = bf16[512,2048]{1,0:T(8,128)(2,1)} fusion(bf16[384,2048]{1,0:T(8,128)(2,1)S(1)} %copy-done, bf16[2048,384]{1,0:T(8,128)(2,1)} %param.35, f32[512,384]{1,0:T(8,128)S(1)} %fusion.66, f32[2048]{0:T(1024)S(1)} %copy-done.21, f32[512]{0:T(512)S(1)} %add_rsqrt_fusion.1, bf16[512,2048]{1,0:T(8,128)(2,1)} %all-gather.4.cloned.1.call-done, ...), kind=kOutput, calls=%fused_computation.23 | convolution fusion | flops 1619132416 | bytes 10233856 | tf_op jit(solution)/shard_map/dot_general | solution.py:251
  337.6 84.6 %all-reduce.2.cloned.1.call-done = bf16[512,2048]{1,0:T(8,128)(2,1)} async-done(((bf16[512,2048]{1,0:T(8,128)(2,1)}), bf16[512,2048]{1,0:T(8,128)(2,1)}) %all-reduce.2.cloned.1.call-update) | async-done | bytes 2097168 | tf_op jit(solution)/shard_map/psum | solution.py:250
  422.3 1.9 convert_add_fusion.1
  (101 shorter events, 13.8 us)
Async XLA Ops:
  7.2 322.4 %copy-start = (bf16[384,2048]{1,0:T(8,128)(2,1)S(1)}, bf16[384,2048]{1,0:T(8,128)(2,1)}, u32[]{:S(2)}) copy-start(bf16[384,2048]{1,0:T(8,128)(2,1)} %param.36) | copy-start | bytes 4718596
  7.2 78.2 %all-gather.4.cloned.1.call-start = ((), (), s32[]{:S(2)}) async-start(), calls=%async_computation.2 | async-start | bytes 2359296 | tf_op jit(solution)/shard_map/all_gather | solution.py:184
  11.1 5.8 %copy-start.15 = (s32[2]{0:T(128)S(1)}, s32[2]{0:T(128)}, u32[]{:S(2)}) copy-start(s32[2]{0:T(128)} %param.41) | copy-start | bytes 28
  11.1 5.9 %copy-start.12 = (s32[1,512]{1,0:T(1,128)S(1)}, s32[1,512]{1,0:T(1,128)}, u32[]{:S(2)}) copy-start(s32[1,512]{1,0:T(1,128)} %param.45) | copy-start | bytes 6148
  11.1 5.9 %copy-start.14 = (s32[2]{0:T(128)S(1)}, s32[2]{0:T(128)}, u32[]{:S(2)}) copy-start(s32[2]{0:T(128)} %param.43) | copy-start | bytes 28
  11.1 6.0 %copy-start.19 = (s32[2]{0:T(128)S(1)}, s32[2]{0:T(128)}, u32[]{:S(2)}) copy-start(s32[2]{0:T(128)} %param.42) | copy-start | bytes 28
  11.1 38.0 %all-to-all-start.1 = ((bf16[64,16,8,128]{3,1,0,2:T(8,128)(2,1)}), bf16[64,16,8,128]{3,1,0,2:T(8,128)(2,1)}, u32[]{:S(2)}, u32[]{:S(2)}) async-start(bf16[64,16,8,128]{3,1,0,2:T(8,128)(2,1)} %copy.39), calls=%async_computation.1 | async-start | bytes 4194304 | tf_op jit(solution)/shard_map/all_to_all | solution.py:214
  17.2 3.8 copy-start.16
  49.1 54.6 %all-to-all-start = ((bf16[64,16,8,128]{3,1,0,2:T(8,128)(2,1)}), bf16[64,16,8,128]{3,1,0,2:T(8,128)(2,1)}, u32[]{:S(2)}, u32[]{:S(2)}) async-start(bf16[64,16,8,128]{3,1,0,2:T(8,128)(2,1)} %copy.36), calls=%async_computation | async-start | bytes 4194304 | tf_op jit(solution)/shard_map/all_to_all | solution.py:213
  54.9 32.7 %copy-start.10 = (f32[2048]{0:T(1024)S(1)}, f32[2048]{0:T(1024)}, u32[]{:S(2)}) copy-start(f32[2048]{0:T(1024)} %param.25) | copy-start | bytes 24580
  54.9 257.4 %all-gather.6.cloned.1.call-start = ((), (), s32[]{:S(2)}) async-start(), calls=%async_computation.4 | async-start | bytes 18874368 | tf_op jit(solution)/shard_map/all_gather | solution.py:243
  85.3 2.2 copy-start.2
  90.2 2.8 copy-start.17
  93.2 3.2 copy-start.18
  97.4 4.0 copy-start.9
  107.7 4.9 %copy-start.13 = (bf16[2,4,1,128]{3,1,2,0:T(4,128)(2,1)S(1)}, bf16[2,4,1,128]{3,1,2,0:T(4,128)(2,1)}, u32[]{:S(2)}) copy-start(bf16[2,4,1,128]{3,1,2,0:T(4,128)(2,1)} %param.39) | copy-start | bytes 6148
  107.7 5.2 %copy-start.5 = (pred[2,256,4096]{1,2,0:T(8,128)(4,1)S(1)}, pred[2,256,4096]{1,2,0:T(8,128)(4,1)}, u32[]{:S(2)}) copy-start(pred[2,256,4096]{1,2,0:T(8,128)(4,1)} %or_and_fusion) | copy-start | bytes 6291460
  117.0 5.7 %copy-start.4 = (f32[2,4096,256,2]{2,1,3,0:T(8,128)}, f32[2,4096,256,2]{2,1,3,0:T(8,128)S(1)}, u32[]{:S(2)}) copy-start(f32[2,4096,256,2]{2,1,3,0:T(8,128)S(1)} %get-tuple-element.31) | copy-start | bytes 50331652
  122.7 9.8 %copy-start.22 = (bf16[2,4,1,128]{3,1,2,0:T(4,128)(2,1)S(1)}, bf16[2,4,1,128]{3,1,2,0:T(4,128)(2,1)}, u32[]{:S(2)}) copy-start(bf16[2,4,1,128]{3,1,2,0:T(4,128)(2,1)} %param.40) | copy-start | bytes 6148
  136.0 286.3 %all-reduce.2.cloned.1.call-start = ((), (), s32[]{:S(2)}) async-start(), calls=%async_computation.3 | async-start | bytes 4194304 | tf_op jit(solution)/shard_map/psum | solution.py:250
  323.3 5.0 %copy-start.3 = (bf16[512,2048]{1,0:T(8,128)(2,1)S(1)}, bf16[512,2048]{1,0:T(8,128)(2,1)}, u32[]{:S(2)}) copy-start(bf16[512,2048]{1,0:T(8,128)(2,1)} %all-gather.4.cloned.1.call-done) | copy-start | bytes 6291460
  323.3 5.0 %copy-start.6 = (bf16[512,2048]{1,0:T(8,128)(2,1)S(1)}, bf16[512,2048]{1,0:T(8,128)(2,1)}, u32[]{:S(2)}) copy-start(bf16[512,2048]{1,0:T(8,128)(2,1)} %reduce_sum.81) | copy-start | bytes 6291460
  323.3 5.0 %copy-start.20 = (bf16[2048,384]{1,0:T(8,128)(2,1)S(1)}, bf16[2048,384]{1,0:T(8,128)(2,1)}, u32[]{:S(2)}) copy-start(bf16[2048,384]{1,0:T(8,128)(2,1)} %param.34) | copy-start | bytes 4718596
  323.3 5.0 %copy-start.21 = (f32[2048]{0:T(1024)S(1)}, f32[2048]{0:T(1024)}, u32[]{:S(2)}) copy-start(f32[2048]{0:T(1024)} %param.33) | copy-start | bytes 24580
  (4 other events, 5.9 us)
Sparse Core Ops, SparseCore 0:
  9.8 75.5 all-gather.3
  136.1 176.0 all-gather.5
  336.2 86.0 all-reduce.1
